TPU v7x, 32 devices: a whole 2x2x4 slice. The times are simulated.
32 devices in a mesh: seq: 8 (over y, x, core), sub: 4 (over z).
Axes of the slice: x: 2, y: 2, z: 4, core: 2. Of those that a mesh axis runs over, the one named last changes fastest.
Arguments:
- query_rows: bfloat16 [8192, 1120], P(('seq', 'sub')), may hold values from -6 to 6
- key_rows: bfloat16 [8192, 1120], P(('seq', 'sub')), may hold values from -6 to 6
- value_rows: bfloat16 [8192, 1120], P(('seq', 'sub')), may hold values from -6 to 6
- query_tangent: bfloat16 [8192, 1120], P(('seq', 'sub')), may hold values from -6 to 6
- key_tangent: bfloat16 [8192, 1120], P(('seq', 'sub')), may hold values from -6 to 6
- value_tangent: bfloat16 [8192, 1120], P(('seq', 'sub')), may hold values from -6 to 6
- teacher: bfloat16 [8192, 2240], P(('seq', 'sub')), may hold values from -64 to 64
- out_weight: bfloat16 [1120, 2240], replicated, may hold values from -0.1875 to 0.1875
- norm_gain: float32 [1120], replicated, may hold values from 0.1 to 1.9
- clip_length: int32 [1], replicated, may hold values from 4096 to 8192
- block_mask: int32 [128], P(('seq', 'sub')), may hold values 0 or 1
Outputs:
- residual: bfloat16 [8192, 2240], P(('seq', 'sub'))
- grad_query: bfloat16 [8192, 1120], P(('seq', 'sub'))
- grad_key: bfloat16 [8192, 1120], P(('seq', 'sub'))
- grad_value: bfloat16 [8192, 1120], P(('seq', 'sub'))
All inputs are finite; a program needn't handle non-finite values. No bound on the sum of `block_mask` on one device may be relied on, other than what follows from the above.
Results may differ from a plain program's by a relative error of at most 0.007.
Values may be sent and summed in bfloat16 or wider, within the bound.
A program may use at most 64 MiB of HBM per device.

v0:
```python
import jax
import jax.numpy as jnp
from jax import lax
from jax.sharding import PartitionSpec as P

H = 10
E = 112
BLK = 64


def split_heads(matrix):
    return matrix.reshape(matrix.shape[0], H, E)


def norm_back(unnorm, scale_inv, weighted):
    inner_mean = jnp.mean(unnorm * weighted, axis=-1, keepdims=True)
    return scale_inv * weighted - unnorm * (scale_inv * scale_inv * scale_inv) * inner_mean


def combine_states(stacked):
    totals = lax.psum(stacked, ("seq", "sub"))
    return totals.astype(jnp.bfloat16)


def local(
    query_rows,
    key_rows,
    value_rows,
    query_tangent,
    key_tangent,
    value_tangent,
    teacher,
    out_weight,
    norm_gain,
    clip_length,
    block_mask,
):
    f32 = jnp.float32
    bf16 = jnp.bfloat16
    tok_rows = query_rows.shape[0]
    first_row = (lax.axis_index("seq") * lax.axis_size("sub") + lax.axis_index("sub")) * tok_rows
    position = first_row + lax.iota(jnp.int32, tok_rows)
    block_flags = jnp.broadcast_to(block_mask[:, None], (tok_rows // BLK, BLK)).reshape(tok_rows)
    valid_rows = jnp.where((position < clip_length[0]) & (block_flags == 1), 1.0, 0.0).astype(f32)[
        :, None
    ]
    key_vals = key_rows.astype(f32)
    key_feat = (valid_rows * jnp.maximum(key_vals, 0.0)).astype(bf16)
    key_slope = valid_rows * jnp.where(key_vals > 0, 1.0, 0.0).astype(f32)
    key_dot = (key_slope * key_tangent.astype(f32)).astype(bf16)
    value_heads = split_heads(value_rows)
    feat_keys = split_heads(key_feat)
    state_part = jnp.einsum("the,thf->hef", feat_keys, value_heads, preferred_element_type=f32)
    tangent_part = jnp.einsum(
        "the,thf->hef", split_heads(key_dot), value_heads, preferred_element_type=f32
    ) + jnp.einsum(
        "the,thf->hef", feat_keys, split_heads(value_tangent), preferred_element_type=f32
    )
    states = combine_states(jnp.stack([state_part, tangent_part]))
    state = states[0]
    state_dot = states[1]
    query_vals = query_rows.astype(f32)
    query_feat = jnp.maximum(query_vals, 0.0).astype(bf16)
    query_slope = jnp.where(query_vals > 0, 1.0, 0.0).astype(f32)
    query_dot = (query_slope * query_tangent.astype(f32)).astype(bf16)
    feat_heads = split_heads(query_feat)
    unnorm = jnp.einsum("the,hef->thf", feat_heads, state, preferred_element_type=f32)
    unnorm_dot = jnp.einsum(
        "the,hef->thf", split_heads(query_dot), state, preferred_element_type=f32
    ) + jnp.einsum("the,hef->thf", feat_heads, state_dot, preferred_element_type=f32)
    gain_heads = norm_gain.reshape(H, E)
    scale_inv = lax.rsqrt(jnp.mean(unnorm * unnorm, axis=-1, keepdims=True) + 1e-06)
    normed_dot = (
        (gain_heads * norm_back(unnorm, scale_inv, unnorm_dot))
        .astype(bf16)
        .reshape(tok_rows, H * E)
    )
    velocity = jnp.dot(normed_dot, out_weight, preferred_element_type=f32)
    residual = (velocity - teacher.astype(f32)).astype(bf16)
    normed_grad = lax.dot_general(
        residual, out_weight, (((1,), (1,)), ((), ())), preferred_element_type=f32
    )
    unnorm_grad = norm_back(unnorm, scale_inv, gain_heads * split_heads(normed_grad)).astype(bf16)
    grad_part = jnp.einsum("the,thf->hef", feat_heads, unnorm_grad, preferred_element_type=f32)
    state_grad = combine_states(grad_part[None])[0]
    grad_query = (
        query_slope
        * jnp.einsum("thf,hef->the", unnorm_grad, state, preferred_element_type=f32).reshape(
            tok_rows, H * E
        )
    ).astype(bf16)
    grad_key = (
        key_slope
        * jnp.einsum("thf,hef->the", value_heads, state_grad, preferred_element_type=f32).reshape(
            tok_rows, H * E
        )
    ).astype(bf16)
    grad_value = (
        jnp.einsum("the,hef->thf", feat_keys, state_grad, preferred_element_type=f32)
        .reshape(tok_rows, H * E)
        .astype(bf16)
    )
    return (residual, grad_query, grad_key, grad_value)


def solution(mesh):
    return jax.shard_map(
        local,
        mesh=mesh,
        in_specs=(
            P(("seq", "sub"), None),
            P(("seq", "sub"), None),
            P(("seq", "sub"), None),
            P(("seq", "sub"), None),
            P(("seq", "sub"), None),
            P(("seq", "sub"), None),
            P(("seq", "sub"), None),
            P(),
            P(),
            P(),
            P(("seq", "sub")),
        ),
        out_specs=(
            P(("seq", "sub"), None),
            P(("seq", "sub"), None),
            P(("seq", "sub"), None),
            P(("seq", "sub"), None),
        ),
        check_vma=False,
    )
```

profile of v0, /device:TPU:0, one launch (start us, length us, event | category | flops | bytes accessed | tf_op | source)
XLA Modules:
  0.0 119.9 jit_solution(6810560053801250112)
XLA Ops:
  0.6 0.0 copy-start
  1.4 0.4 copy-done
  1.7 0.7 broadcast_compare_fusion
  2.4 0.1 broadcast_in_dim.29
  2.4 0.1 eq.16
  2.5 0.8 mul.117
  3.3 1.6 %fusion.4 = (bf16[256,1120]{0,1:T(8,128)(2,1)S(1)}, bf16[256,1120]{0,1:T(8,128)(2,1)S(1)}) fusion(bf16[256,1120]{0,1:T(8,128)(2,1)} %param.12, f32[256]{0:T(256)S(1)} %and_select_fusion, bf16[256,1120]{0,1:T(8,128)(2,1)} %param.15), kind=kLoop, calls=%fused_computation.17 | loop fusion | flops 2867200 | bytes 2294784 | tf_op jit(solution)/shard_map/convert_element_type | solution.py:48
  4.9 0.0 copy-start.3
  5.0 0.3 fusion.16
  5.3 0.7 copy-done.3
  6.0 0.3 fusion.2
  6.3 0.3 convolution_bitcast_fusion.2
  6.6 0.1 pad_maximum_fusion
  6.7 0.0 copy-start.1
  6.7 53.7 %all-reduce.2 = bf16[2,10,112,112]{3,2,1,0:T(8,128)(2,1)S(1)} all-reduce(f32[2,10,112,112]{3,2,1,0:T(8,128)S(1)} %pad_maximum_fusion), channel_id=1, replica_groups=mesh['seq'=8,'sub'=4] {'seq','sub'}, use_global_device_ids=true, to_apply=%region_0.1 | all-reduce | flops 250880 | bytes 1505280 | tf_op jit(solution)/shard_map/psum | solution.py:21
  60.4 0.0 copy-done.1
  60.5 0.0 slice-start
  60.5 1.5 %fusion.5 = (bf16[256,1120]{0,1:T(8,128)(2,1)S(1)}, bf16[256,1120]{0,1:T(8,128)(2,1)S(1)}) fusion(bf16[256,1120]{0,1:T(8,128)(2,1)S(1)} %copy-done.1, bf16[256,1120]{0,1:T(8,128)(2,1)} %param.14), kind=kLoop, calls=%fused_computation.18 | loop fusion | flops 2293760 | bytes 2293760 | tf_op jit(solution)/shard_map/convert_element_type | solution.py:63
  61.9 0.4 fusion.13
  62.3 0.0 slice-start.1
  62.3 0.4 fusion.1
  62.7 0.4 multiply_reduce_fusion.2
  63.1 0.0 copy-start.4
  63.1 0.6 multiply_convert_fusion
  63.7 0.0 slice-done
  63.7 0.0 slice-done.1
  63.7 0.7 copy-done.4
  64.5 2.3 %fusion = bf16[256,2240]{0,1:T(8,128)(2,1)S(1)} fusion(bf16[256,1120]{0,1:T(8,128)(2,1)S(1)} %bitcast.81, bf16[1120,2240]{1,0:T(8,128)(2,1)S(1)} %bitcast.83, bf16[256,2240]{0,1:T(8,128)(2,1)S(1)} %copy-done.4), kind=kOutput, calls=%fused_computation.1 | convolution fusion | flops 1286225920 | bytes 7884800 | tf_op jit(solution)/shard_map/dot_general | solution.py:78
  66.8 0.0 copy-start.5
  66.8 1.5 %fusion.17 = f32[256,1120]{0,1:T(8,128)S(1)} fusion(bf16[1120,2240]{1,0:T(8,128)(2,1)S(1)} %bitcast.83, bf16[256,2240]{0,1:T(8,128)(2,1)S(1)} %fusion), kind=kOutput, calls=%fused_computation.47 | convolution fusion | flops 1284505600 | bytes 7311360 | tf_op jit(solution)/shard_map/dot_general | solution.py:80
  68.3 0.0 copy-done.5
  68.3 0.2 multiply_reduce_fusion
  68.6 0.3 subtract_convert_fusion
  68.9 0.3 convolution_bitcast_fusion.1
  69.2 0.3 fusion.12
  69.5 1.0 fusion.7
  70.5 46.1 %all-reduce.3 = bf16[1,10,112,112]{3,2,1,0:T(8,128)(2,1)S(1)} all-reduce(f32[1,10,112,112]{3,2,1,0:T(8,128)S(1)} %convolution_bitcast_fusion.1), channel_id=1, replica_groups=mesh['seq'=8,'sub'=4] {'seq','sub'}, use_global_device_ids=true, to_apply=%region_4.5 | all-reduce | flops 125440 | bytes 752640 | tf_op jit(solution)/shard_map/psum | solution.py:21
  116.6 1.2 convolution_convert_fusion
  117.8 0.0 copy-start.2
  117.8 0.3 fusion.10
  118.1 0.8 copy-done.2
  118.9 1.0 fusion.8
  (4 shorter events, 0.0 us)
Async XLA Ops:
  0.6 1.1 copy-start
  4.9 1.1 copy-start.3
  6.7 53.7 %copy-start.1 = (bf16[256,1120]{0,1:T(8,128)(2,1)S(1)}, bf16[256,1120]{0,1:T(8,128)(2,1)}, u32[]{:S(2)}) copy-start(bf16[256,1120]{0,1:T(8,128)(2,1)} %param.11) | copy-start | bytes 1720324
  60.5 3.3 %slice-start = ((s8[5160960]{0:T(1024)(128)(4,1)}), s8[4194304]{0:T(1024)(128)(4,1)S(1)}, s32[]{:S(2)}) async-start(s8[5160960]{0:T(1024)(128)(4,1)} %bitcast.82), calls=%async_computation | async-start | bytes 8388608
  62.3 1.4 %slice-start.1 = ((s8[5160960]{0:T(1024)(128)(4,1)}), s8[966656]{0:T(1024)(128)(4,1)S(1)}, s32[]{:S(2)}) async-start(s8[5160960]{0:T(1024)(128)(4,1)} %bitcast.82), calls=%async_computation.1 | async-start | bytes 1933312
  63.1 1.3 %copy-start.4 = (bf16[256,2240]{0,1:T(8,128)(2,1)S(1)}, bf16[256,2240]{0,1:T(8,128)(2,1)}, u32[]{:S(2)}) copy-start(bf16[256,2240]{0,1:T(8,128)(2,1)} %param.17) | copy-start | bytes 3440644
  66.8 1.5 %copy-start.5 = (bf16[256,2240]{0,1:T(8,128)(2,1)}, bf16[256,2240]{0,1:T(8,128)(2,1)S(1)}, u32[]{:S(2)}) copy-start(bf16[256,2240]{0,1:T(8,128)(2,1)S(1)} %fusion) | copy-start | bytes 3440644
  117.8 1.1 copy-start.2
where the time goes:
time: 120 us
  blocking collectives  99.8 us (83%)
  matrix products  7.92 us (7%)
  other arithmetic  7.01 us (6%)
  local copies, waits for them, and re-layouts  3.56 us (3%)
  between operations  1.56 us (1%)
    psum x2, blocking collectives, combine_states(): totals = lax.psum(stacked, ('seq', 'sub'))  99.8 us
    unnamed x16, local copies, waits for them, and re-layouts  2.62 us

commit v1 on v0

--- a/solution.py
+++ b/solution.py
@@ -18,7 +18,7 @@
 
 
 def combine_states(stacked):
-    totals = lax.psum(stacked, ("seq", "sub"))
+    totals = lax.psum(lax.psum(stacked, "seq"), "sub")
     return totals.astype(jnp.bfloat16)
 
 

time: 120 us -> 226 us (1.88)
  waiting for transfers between devices: 0 us -> 109 us
  blocking collectives: 99.8 us -> 77.7 us
  between operations: 1.56 us -> 15 us
  matrix products: 7.92 us -> 12.5 us
    psum x0 -> x2, waiting for transfers between devices: none -> 109 us  [combine_states(): totals = lax.psum(lax.psum(stacked, 'seq'), 'sub')]
    psum x2, blocking collectives: 99.8 us -> 77.7 us  [combine_states(): totals = lax.psum(lax.psum(stacked, 'seq'), 'sub')]
    dot_general x1, matrix products: 2.33 us -> 5.08 us  [local(): velocity = jnp.dot(normed_dot, out_weight, preferred_element_type=f32)]
  transfers between devices with their start and end apart: 0 -> 2, of which waited for: 0 -> 2; matrix products, arithmetic and copies ran while one was open for 0% -> 1% of each run, Pallas kernels for 0% -> 0%
where the time goes in v1:
time: 226 us
  waiting for transfers between devices  109 us (48%)
  blocking collectives  77.7 us (34%)
  between operations  15 us (7%)
  matrix products  12.5 us (6%)
  other arithmetic  8.03 us (4%)
  local copies, waits for them, and re-layouts  3.14 us (1%)
    psum x2, waiting for transfers between devices, combine_states(): totals = lax.psum(lax.psum(stacked, 'seq'), 'sub')  109 us
    psum x2, blocking collectives, combine_states(): totals = lax.psum(lax.psum(stacked, 'seq'), 'sub')  77.7 us
    dot_general x1, matrix products, local(): velocity = jnp.dot(normed_dot, out_weight, preferred_element_type=f32)  5.08 us
  transfers between devices with their start and end apart: 2, of which 2 were waited for; matrix products, arithmetic and copies ran while one was open for 1% of the time, Pallas kernels for 0%

profile of v1, /device:TPU:0, one launch (start us, length us, event | category | flops | bytes accessed | tf_op | source)
XLA Modules:
  0.0 225.7 jit_solution(6961558122113905233)
XLA Ops:
  7.2 0.0 copy-start
  7.2 0.0 all-reduce.5.cloned.1.call-start
  7.9 0.7 broadcast_compare_fusion
  8.6 0.1 broadcast_in_dim.29
  8.7 0.1 eq.16
  8.8 1.6 fusion.4
  10.4 0.0 copy-done
  10.4 0.3 fusion.16
  10.7 0.0 copy-start.3
  10.7 0.3 convolution_bitcast_fusion.2
  11.0 0.7 copy-done.3
  11.8 0.3 fusion.2
  12.1 0.0 copy-start.5
  12.1 1.1 pad_maximum_fusion
  13.2 0.0 all-reduce.5.cloned.1.call-update
  13.2 0.0 all-reduce.7.cloned.1.call-start
  13.2 0.0 copy-done.5
  13.3 0.1 mul.117
  13.3 0.9 copy-done.1
  14.2 0.2 copy-done.4
  14.4 0.3 fusion.5
  14.7 58.5 %all-reduce.5.cloned.1.call-done = f32[2,10,112,112]{3,2,1,0:T(8,128)} async-done(((f32[2,10,112,112]{3,2,1,0:T(8,128)}), f32[2,10,112,112]{3,2,1,0:T(8,128)}) %all-reduce.5.cloned.1.call-update) | async-done | bytes 1003536 | tf_op jit(solution)/shard_map/psum | solution.py:21
  73.2 46.1 %all-reduce.8 = bf16[2,10,112,112]{3,2,1,0:T(8,128)(2,1)S(1)} all-reduce(f32[2,10,112,112]{3,2,1,0:T(8,128)} %all-reduce.5.cloned.1.call-done), channel_id=1, replica_groups=mesh['seq'=8,'sub'=4] {'sub'}, use_global_device_ids=true, to_apply=%region_1.2 | all-reduce | flops 250880 | bytes 1505280 | tf_op jit(solution)/shard_map/psum | solution.py:21
  119.3 0.4 fusion.13
  119.7 0.4 fusion.1
  120.1 0.0 copy-start.6
  120.1 0.4 multiply_reduce_fusion.2
  120.5 0.0 slice-start
  120.5 0.5 multiply_convert_fusion
  121.0 0.3 copy-done.6
  121.3 5.1 %fusion = bf16[256,2240]{0,1:T(8,128)(2,1)S(1)} fusion(bf16[256,1120]{0,1:T(8,128)(2,1)S(1)} %bitcast.81, bf16[1120,2240]{1,0:T(8,128)(2,1)} %param.18, bf16[256,2240]{0,1:T(8,128)(2,1)S(1)} %copy-done.6), kind=kOutput, calls=%fused_computation.1 | convolution fusion | flops 1286225920 | bytes 7884800 | tf_op jit(solution)/shard_map/dot_general | solution.py:78
  126.4 0.0 slice-done
  126.4 0.0 slice-done.1
  126.4 0.0 copy-start.7
  126.5 1.5 fusion.17
  128.0 0.0 copy-done.7
  128.0 0.2 multiply_reduce_fusion
  128.2 0.3 subtract_convert_fusion
  128.5 1.1 convolution_bitcast_fusion.1
  129.6 1.3 fusion.12
  130.9 0.0 all-reduce.7.cloned.1.call-update
  131.0 2.3 %fusion.7 = bf16[256,1120]{0,1:T(8,128)(2,1)} fusion(f32[10,112,256]{2,1,0:T(8,128)} %fusion.12, bf16[256,1120]{0,1:T(8,128)(2,1)S(1)} %copy-done.1), kind=kLoop, calls=%fused_computation.20 | loop fusion | flops 1433600 | bytes 2293760 | tf_op jit(solution)/shard_map/convert_element_type | solution.py:91
  133.2 50.8 %all-reduce.7.cloned.1.call-done = f32[1,10,112,112]{3,2,1,0:T(8,128)} async-done(((f32[1,10,112,112]{3,2,1,0:T(8,128)}), f32[1,10,112,112]{3,2,1,0:T(8,128)}) %all-reduce.7.cloned.1.call-update) | async-done | bytes 501776 | tf_op jit(solution)/shard_map/psum | solution.py:21
  184.0 31.6 %all-reduce.9 = bf16[1,10,112,112]{3,2,1,0:T(8,128)(2,1)S(1)} all-reduce(f32[1,10,112,112]{3,2,1,0:T(8,128)} %all-reduce.7.cloned.1.call-done), channel_id=1, replica_groups=mesh['seq'=8,'sub'=4] {'sub'}, use_global_device_ids=true, to_apply=%region_6.7 | all-reduce | flops 125440 | bytes 752640 | tf_op jit(solution)/shard_map/psum | solution.py:21
  215.6 1.2 convolution_convert_fusion
  216.8 0.3 fusion.10
  217.1 0.8 copy-done.2
  217.8 1.0 fusion.8
  (8 shorter events, 0.0 us)
Async XLA Ops:
  7.2 3.2 %copy-start = (bf16[256,1120]{0,1:T(8,128)(2,1)S(1)}, bf16[256,1120]{0,1:T(8,128)(2,1)}, u32[]{:S(2)}) copy-start(bf16[256,1120]{0,1:T(8,128)(2,1)} %param.13) | copy-start | bytes 1720324
  7.2 66.0 %all-reduce.5.cloned.1.call-start = ((), (), s32[]{:S(2)}) async-start(), calls=%async_computation | async-start | bytes 2293760 | tf_op jit(solution)/shard_map/psum | solution.py:21
  10.7 1.1 copy-start.3
  12.1 1.2 copy-start.5
  13.2 1.1 copy-start.1
  13.2 1.2 copy-start.4
  13.2 170.8 %all-reduce.7.cloned.1.call-start = ((), (), s32[]{:S(2)}) async-start(), calls=%async_computation.1 | async-start | bytes 1146880 | tf_op jit(solution)/shard_map/psum | solution.py:21
  120.1 1.3 copy-start.6
  120.5 5.9 %slice-start = ((s8[5160960]{0:T(1024)(128)(4,1)}), s8[4194304]{0:T(1024)(128)(4,1)S(1)}, s32[]{:S(2)}) async-start(s8[5160960]{0:T(1024)(128)(4,1)} %bitcast.82), calls=%async_computation.2 | async-start | bytes 8388608
  121.3 5.1 %slice-start.1 = ((s8[5160960]{0:T(1024)(128)(4,1)}), s8[966656]{0:T(1024)(128)(4,1)S(1)}, s32[]{:S(2)}) async-start(s8[5160960]{0:T(1024)(128)(4,1)} %bitcast.82), calls=%async_computation.3 | async-start | bytes 1933312
  126.4 1.5 copy-start.7
  216.8 1.1 copy-start.2
Sparse Core Ops, SparseCore 0:
  13.3 59.8 all-reduce.4
  131.1 52.8 all-reduce.6
